TPU v7x, 32 devices: a whole 2x2x4 slice. The times are simulated.
32 devices in a mesh: groups: 1, ctx: 16 (over z, y, core), pipe: 2 (over x), dp: 1.
Axes of the slice: x: 2, y: 2, z: 4, core: 2. Of those that a mesh axis runs over, the one named last changes fastest.
Arguments:
- rows_in: bfloat16 [2, 1, 4096, 1024], P(('groups', 'pipe'), 'dp', 'ctx'), may hold values from -6 to 6
- queries: bfloat16 [2, 1, 4096, 1024], P(('groups', 'pipe'), 'dp', 'ctx'), may hold values from -6 to 6
- keys: bfloat16 [2, 1, 4096, 1024], P(('groups', 'pipe'), 'dp', 'ctx'), may hold values from -12 to 12
- strengths: float32 [2, 1, 8, 4096], P(('groups', 'pipe'), 'dp', None, 'ctx'), may hold values from 0.05 to 0.5
- gates: float32 [2, 1, 8, 4096], P(('groups', 'pipe'), 'dp', None, 'ctx'), may hold values from 0.45 to 1
- doc_ids: int32 [2, 1, 4096], P(('groups', 'pipe'), 'dp', 'ctx'), may hold values from 0 to 7, never falling along the last dimension, each value on 1 to 1024 neighbouring positions
- positives: int32 [2, 1, 8], P(('groups', 'pipe'), 'dp'), may hold values from 0 to 7, as said below
- norm_gain: float32 [2, 128], P('pipe'), may hold values from 0.5 to 1.5
Outputs:
- rows_next: bfloat16 [2, 1, 4096, 1024], P(('groups', 'pipe'), 'dp', 'ctx')
- doc_loss: float32 [2, 1, 8], P(('groups', 'pipe'), 'dp')
Inputs may be any that keep to these rules, and one draw needn't show every extreme that they name: `positives`: never the document's own index dp * 8 + its document number.
All inputs are finite; a program needn't handle non-finite values.
Results may differ from a plain program's by a relative error of at most 0.008.
Values may be sent and summed in bfloat16 or wider, within the bound.
No kernel may reach another device: no remote copies, remote signals or barrier semaphores. Data moves between devices by JAX's collectives and lax.ppermute only.
A program may use at most 128 MiB of HBM per device.

v0:
```python
import jax
import jax.numpy as jnp
from jax import lax
from jax.sharding import PartitionSpec as P


def from_behind(block, axis, distance):
    devices = range(lax.axis_size(axis))
    route = [(i - distance, i) for i in devices if i - distance in devices]
    return lax.ppermute(block, axis, route)


def entering(array, axis, combine, identity):
    size, place = (lax.axis_size(axis), lax.axis_index(axis))
    everything = jax.tree.map(
        lambda part, kind: lax.all_gather(part.astype(kind), axis),
        array,
        (jnp.bfloat16, jnp.bfloat16),
    )
    start = jax.tree.map(
        lambda part, zero: jnp.broadcast_to(jnp.asarray(zero, part.dtype), part.shape),
        array,
        identity,
    )

    def step(k, before):
        reached = k < place
        new = combine(
            before, jax.tree.map(lambda part, own: part[k].astype(own.dtype), everything, array)
        )
        return jax.tree.map(lambda a, b: jnp.where(reached, a, b), new, before)

    return lax.fori_loop(0, size, step, start)


def shifted(array, axis, by):
    size = lax.axis_size(axis)
    return lax.ppermute(array, axis, [(i, (i + by) % size) for i in range(size)])


def unit_rows(x):
    return x * lax.rsqrt(jnp.sum(x * x, axis=-1, keepdims=True) + 1e-06)


def on_device(rows_in, queries, keys, strengths, gates, doc_ids, positives, norm_gain):
    hi = lax.Precision.HIGHEST
    length = rows_in.shape[2]
    heads = strengths.shape[2]
    width = rows_in.shape[3] // heads
    ndoc = positives.shape[2]
    values = rows_in[0, 0].astype(jnp.float32).reshape(length, heads, width).transpose(1, 0, 2)
    qn = unit_rows(
        queries[0, 0].astype(jnp.float32).reshape(length, heads, width).transpose(1, 0, 2)
    )
    kn = unit_rows(keys[0, 0].astype(jnp.float32).reshape(length, heads, width).transpose(1, 0, 2))
    beta = strengths[0, 0]
    ids = doc_ids[0, 0]
    before = from_behind(ids[-1:], "ctx", 1)
    prior = jnp.concatenate([before, ids[:-1]])
    reset = (ids != prior).astype(jnp.int32)
    run = jnp.cumsum(reset)
    logsum = jnp.cumsum(jnp.log(gates[0, 0]), axis=1)
    rows_idx = jnp.arange(length)[:, None]
    cols_idx = jnp.arange(length)[None, :]
    same = (run[:, None] == run[None, :]) & (rows_idx >= cols_idx)
    expo = jnp.where(same[None], logsum[:, :, None] - logsum[:, None, :], -jnp.inf)
    decay = jnp.exp(expo)
    lead = jnp.exp(logsum) * (run == 0).astype(jnp.float32)[None, :]
    tail = decay[:, length - 1, :]
    lead_end = lead[:, length - 1]
    inner = jnp.einsum("hti,hsi->hts", kn, kn, precision=hi)
    lower = jnp.where((rows_idx > cols_idx)[None], beta[:, :, None] * decay * inner, 0.0)
    eye_long = jnp.eye(length, dtype=jnp.float32)
    system = lower + eye_long[None]
    rhs = jnp.concatenate([beta[..., None] * values, (beta * lead)[..., None] * kn], axis=2)
    solved = jax.scipy.linalg.solve_triangular(system, rhs, lower=True, unit_diagonal=True)
    wv = solved[:, :, :width]
    yy = solved[:, :, width:]
    kd = kn * tail[..., None]
    eye_small = jnp.eye(width, dtype=jnp.float32)
    pmat = lead_end[:, None, None] * eye_small[None] - jnp.einsum(
        "hti,htj->hij", kd, yy, precision=hi
    )
    umat = jnp.einsum("hti,htj->hij", kd, wv, precision=hi)

    def combine(earlier, later):
        first = jnp.einsum("hij,hjk->hik", later[0], earlier[0], precision=hi)
        second = jnp.einsum("hij,hjk->hik", later[0], earlier[1], precision=hi) + later[1]
        return (first, second)

    identity = (jnp.broadcast_to(eye_small, pmat.shape), jnp.zeros_like(umat))
    prefix = entering((pmat, umat), "ctx", combine, identity)
    state_in = prefix[1]
    writes = wv - jnp.einsum("hti,hij->htj", yy, state_in, precision=hi)
    attend = decay * jnp.einsum("hti,hsi->hts", qn, kn, precision=hi)
    outs = lead[..., None] * jnp.einsum("hti,hij->htj", qn, state_in, precision=hi)
    outs = outs + jnp.einsum("hts,hsj->htj", attend, writes, precision=hi)
    scale = lax.rsqrt(jnp.mean(outs * outs, axis=-1, keepdims=True) + 1e-06)
    normed = outs * scale * norm_gain[0][None, None, :]
    rows_out = (
        (values + normed).transpose(1, 0, 2).reshape(length, heads * width).astype(jnp.bfloat16)
    )
    passed = shifted(rows_out, "pipe", 1)
    onehot = (jnp.arange(ndoc, dtype=jnp.int32)[:, None] == ids[None, :]).astype(jnp.bfloat16)
    pooled = jnp.dot(onehot, rows_out, preferred_element_type=jnp.float32)
    replica = lax.axis_index("dp")
    replicas = lax.axis_size("dp")
    summed = lax.psum(pooled.astype(jnp.bfloat16), "ctx").astype(jnp.float32)
    mine = unit_rows(summed)
    cands = lax.all_gather(mine.astype(jnp.bfloat16), "dp", axis=0, tiled=True).astype(mine.dtype)
    scores = jnp.dot(mine, cands.T, precision=hi, preferred_element_type=jnp.float32) / 0.05
    cidx = jnp.arange(replicas * ndoc, dtype=jnp.int32)
    own = replica * ndoc + jnp.arange(ndoc, dtype=jnp.int32)
    total = jnp.sum(jnp.where(cidx[None, :] != own[:, None], jnp.exp(scores), 0.0), axis=-1)
    picked = jnp.sum(jnp.where(cidx[None, :] == positives[0, 0][:, None], scores, 0.0), axis=-1)
    doc_loss = (jnp.log(total) - picked).reshape(1, 1, ndoc)
    return (passed.reshape(1, 1, length, heads * width), doc_loss)


def solution(mesh):
    in_specs = (
        P(("groups", "pipe"), "dp", "ctx", None),
        P(("groups", "pipe"), "dp", "ctx", None),
        P(("groups", "pipe"), "dp", "ctx", None),
        P(("groups", "pipe"), "dp", None, "ctx"),
        P(("groups", "pipe"), "dp", None, "ctx"),
        P(("groups", "pipe"), "dp", "ctx"),
        P(("groups", "pipe"), "dp", None),
        P("pipe", None),
    )
    out_specs = (P(("groups", "pipe"), "dp", "ctx", None), P(("groups", "pipe"), "dp", None))
    return jax.shard_map(
        on_device, mesh=mesh, in_specs=in_specs, out_specs=out_specs, check_vma=False
    )
```

profile of v0, /device:TPU:0, one launch (start us, length us, event | category | flops | bytes accessed | tf_op | source)
XLA Modules:
  0.0 435.6 jit_solution(13908347986221242588)
XLA Ops:
  7.2 1.3 slice.54
  8.5 2.9 collective-permute-start
  11.5 1.2 copy.35
  14.1 0.7 iota_compare_fusion.2
  15.1 1.2 copy.38
  16.3 1.6 bitcast_multiply_fusion.1
  17.9 0.8 compare_convert_fusion.1
  19.5 1.7 select_exponential_fusion
  21.2 4.0 select_add_fusion
  25.2 8.1 %while.15 = (s32[]{:T(128)}, f32[8,256,256]{2,1,0:T(8,128)}, s32[2,2]{1,0:T(2,128)S(1)}, f32[2,8,128,128]{3,2,0,1:T(8,128)}, s32[]{:T(128)}) while((s32[]{:T(128)}, f32[8,256,256]{2,1,0:T(8,128)}, s32[2,2]{1,0:T(2,128)S(1)}, f32[2,8,128,128]{3,2,0,1:T(8,128)}, s32[]{:T(128)}) %tuple.60), condition=%wide.while_cond, body=%wide.while_body.sunk | while | flops 2 | bytes 1050209 | solution.py:76
  25.8 3.6 bitcast_dynamic-update-slice_fusion.2
  30.0 3.4 bitcast_dynamic-update-slice_fusion.2
  33.4 158.6 %custom-call.4 = f32[8,2,128,128]{2,3,1,0:T(8,128)} custom-call(f32[8,2,128,128]{3,2,1,0:T(8,128)} %bitcast.135), custom_call_target="InvertDiagBlocksLowerTriangular" | custom-call | tf_op jit(solution)/shard_map/jit(_solve_triangular)/vmap()/triangular_solve | solution.py:76
  192.6 0.6 copy-done.6
  193.2 1.0 fusion.13
  194.3 2.1 convolution_subtract_fusion.1
  196.4 1.0 fusion.33
  197.4 0.8 slice.79
  198.3 3.4 convolution_convert_fusion
  202.1 3.4 fusion.10
  205.5 1.1 convert_bitcast_fusion
  207.2 0.6 copy-done.1
  207.8 3.3 fusion.25
  211.2 43.2 %all-gather.7.cloned.1.call-done = bf16[128,128,128]{2,1,0:T(8,128)(2,1)} async-done(((bf16[8,128,128]{2,1,0:T(8,128)(2,1)}), bf16[128,128,128]{2,1,0:T(8,128)(2,1)}) %all-gather.7.cloned.1.call-update) | async-done | bytes 4194320 | tf_op jit(solution)/shard_map/all_gather | solution.py:16
  254.4 51.2 %all-gather.5.cloned.1.call-done = bf16[128,128,128]{2,1,0:T(8,128)(2,1)} async-done(((bf16[8,128,128]{2,1,0:T(8,128)(2,1)}), bf16[128,128,128]{2,1,0:T(8,128)(2,1)}) %all-gather.5.cloned.1.call-update) | async-done | bytes 4194320 | tf_op jit(solution)/shard_map/all_gather | solution.py:16
  305.6 53.4 %while.16 = (s32[]{:T(128)}, f32[8,128,128]{2,1,0:T(8,128)}, s32[]{:T(128)}, bf16[16,8,128,128]{3,2,1,0:T(8,128)(2,1)}, bf16[16,8,128,128]{3,2,1,0:T(8,128)(2,1)}, /*index=5*/s32[]{:T(128)}, s32[]{:T(128)}) while((s32[]{:T(128)}, f32[8,128,128]{2,1,0:T(8,128)}, s32[]{:T(128)}, bf16[16,8,128,128]{3,2,1,0:T(8,128)(2,1)}, ...), condition=%wide.region_7.8_spmd.clone, body=%wide.region_6.7_spmd.clone.sunk | while | flops 201981952 | bytes 3148383 | solution.py:33
  305.6 1.0 copy.89
  306.7 2.3 fusion.72
  309.0 1.0 copy.89
  310.0 2.3 fusion.72
  312.3 1.0 copy.89
  313.3 2.3 fusion.72
  315.6 1.0 copy.89
  316.7 2.3 fusion.72
  319.0 1.0 copy.89
  320.0 2.3 fusion.72
  322.3 1.0 copy.89
  323.4 2.3 fusion.72
  325.6 1.0 copy.89
  326.7 2.3 fusion.72
  329.0 1.0 copy.89
  330.0 2.3 fusion.72
  332.3 1.0 copy.89
  333.4 2.3 fusion.72
  335.7 1.0 copy.89
  336.7 2.3 fusion.72
  339.0 1.0 copy.89
  340.0 2.3 fusion.72
  342.3 1.0 copy.89
  343.4 2.3 fusion.72
  345.7 1.0 copy.89
  346.7 2.3 fusion.72
  349.0 1.0 copy.89
  350.0 2.3 fusion.72
  352.3 1.0 copy.89
  353.4 2.3 fusion.72
  355.7 1.0 copy.89
  356.7 2.3 fusion.72
  359.0 2.2 convolution_subtract_fusion
  361.3 1.5 fusion.26
  362.9 2.8 multiply_reduce_fusion
  366.2 1.5 collective-permute-start.1
  367.9 58.9 %psum.7 = bf16[8,1024]{1,0:T(8,128)(2,1)S(1)} all-reduce(bf16[8,1024]{1,0:T(8,128)(2,1)S(1)} %convolution_convert_fusion.1), channel_id=1, replica_groups=mesh['groups'=1,'ctx'=16,'pipe'=2,'dp'=1] {'ctx'}, use_global_device_ids=true, to_apply=%region_9.10 | all-reduce | flops 8192 | bytes 32768 | tf_op jit(solution)/shard_map/psum | solution.py:108
  427.7 1.0 copy.45
  (73 shorter events, 6.9 us)
Async XLA Ops:
  7.2 6.2 %copy-start.12 = (f32[1,1,8,256]{3,2,1,0:T(8,128)S(1)}, f32[1,1,8,256]{3,2,1,0:T(8,128)}, u32[]{:S(2)}) copy-start(f32[1,1,8,256]{3,2,1,0:T(8,128)} %param.14) | copy-start | bytes 24580
  7.2 7.7 %copy-start.7 = (bf16[1,1,256,1024]{3,2,1,0:T(8,128)(2,1)S(1)}, bf16[1,1,256,1024]{3,2,1,0:T(8,128)(2,1)}, u32[]{:S(2)}) copy-start(bf16[1,1,256,1024]{3,2,1,0:T(8,128)(2,1)} %param.10) | copy-start | bytes 1572868
  7.2 247.2 %all-gather.7.cloned.1.call-start = ((), (), s32[]{:S(2)}) async-start(), calls=%async_computation.1 | async-start | bytes 4456448 | tf_op jit(solution)/shard_map/all_gather | solution.py:16
  8.5 9.4 %collective-permute-start = (s32[1]{0:T(128)}, s32[1]{0:T(128)}, u32[]{:S(2)}, u32[]{:S(2)}) collective-permute-start(s32[1]{0:T(128)} %bitcast.4), channel_id=1, source_target_pairs={{0,2},{2,4},{4,6},{6,8},{8,10},{10,12},{12,14},{14,16},{16,18},{18... | collective-permute-start | bytes 20 | tf_op jit(solution)/shard_map/ppermute | solution.py:10
  13.0 3.3 copy-start.10
  15.1 6.1 %copy-start.4 = (bf16[1,1,256,1024]{2,3,1,0:T(8,128)(2,1)}, bf16[1,1,256,1024]{2,3,1,0:T(8,128)(2,1)S(1)}, u32[]{:S(2)}) copy-start(bf16[1,1,256,1024]{2,3,1,0:T(8,128)(2,1)S(1)} %copy.33) | copy-start | bytes 1572868
  15.1 2.8 copy-start.11
  16.3 4.9 %copy-start.8 = (pred[256,256]{1,0:T(8,128)(4,1)S(1)}, pred[256,256]{1,0:T(8,128)(4,1)}, u32[]{:S(2)}) copy-start(pred[256,256]{1,0:T(8,128)(4,1)} %get-tuple-element.157) | copy-start | bytes 196612
  16.3 4.9 %copy-start.9 = (pred[256,256]{1,0:T(8,128)(4,1)S(1)}, pred[256,256]{1,0:T(8,128)(4,1)}, u32[]{:S(2)}) copy-start(pred[256,256]{1,0:T(8,128)(4,1)} %get-tuple-element.158) | copy-start | bytes 196612
  192.0 1.2 copy-start.6
  201.7 104.0 %all-gather.5.cloned.1.call-start = ((), (), s32[]{:S(2)}) async-start(), calls=%async_computation | async-start | bytes 4456448 | tf_op jit(solution)/shard_map/all_gather | solution.py:16
  206.9 1.0 copy-start.1
  359.0 2.3 copy-start
  359.0 2.3 copy-start.2
  361.3 1.6 copy-start.3
  362.9 2.9 copy-start.5
  362.9 2.9 copy-start.13
  365.7 61.3 %copy-start.14 = (s32[1,1,8]{2,1,0:T(1,128)S(1)}, s32[1,1,8]{2,1,0:T(1,128)}, u32[]{:S(2)}) copy-start(s32[1,1,8]{2,1,0:T(1,128)} %param.16) | copy-start | bytes 100
  366.2 61.6 %collective-permute-start.1 = (bf16[256,1024]{0,1:T(8,128)(2,1)S(1)}, bf16[256,1024]{0,1:T(8,128)(2,1)S(1)}, u32[]{:S(2)}, u32[]{:S(2)}) collective-permute-start(bf16[256,1024]{0,1:T(8,128)(2,1)S(1)} %bitcast.121), channel_id=1, source_target_pairs={{0,1},{1,0},{2,3},{3,2},{4,5},{5,4},{6,7},{7,6},{8,9},{9,8},{10,11... | collective-permute-start | bytes 1572872 | tf_op jit(solution)/shard_map/ppermute | solution.py:38
Sparse Core Ops, SparseCore 0:
  201.8 52.5 all-gather.6
  256.6 49.0 all-gather.4
where the time goes:
time: 437 us; the launch traced here: 436 us
  other arithmetic  168 us (38%)
  waiting for transfers between devices  94.5 us (22%)
  matrix products  61.9 us (14%)
  blocking collectives  58.9 us (13%)
  local copies, waits for them, and re-layouts  33 us (8%)
  between operations  14.4 us (3%)
  starting transfers between devices  4.72 us (1%)
    another operation x4, other arithmetic, on_device(): jax.scipy.linalg.solve_triangular(system, rhs, lower=True, unit_diagonal=...  159 us
    all_gather x2, waiting for transfers between devices, entering(): lax.all_gather(part.astype(kind), axis)  94.5 us
    psum x1, blocking collectives, on_device(): summed = lax.psum(pooled.astype(jnp.bfloat16), 'ctx').astype(jnp.float32)  58.9 us
    dot_general x16, matrix products, combine(): jnp.einsum('hij,hjk->hik', later[0], earlier[1], precision=hi) + later[1]  36.7 us
    while x16, local copies, waits for them, and re-layouts  16.7 us
  transfers between devices with their start and end apart: 4, of which 2 were waited for; matrix products, arithmetic and copies ran while one was open for 4% of the time, Pallas kernels for 0%

commit v1 on v0

--- a/solution.py
+++ b/solution.py
@@ -105,7 +105,7 @@
     pooled = jnp.dot(onehot, rows_out, preferred_element_type=jnp.float32)
     replica = lax.axis_index("dp")
     replicas = lax.axis_size("dp")
-    summed = lax.psum(pooled.astype(jnp.bfloat16), "ctx").astype(jnp.float32)
+    summed = jnp.sum(lax.all_gather(pooled.astype(jnp.bfloat16), "ctx"), axis=0).astype(jnp.float32)
     mine = unit_rows(summed)
     cands = lax.all_gather(mine.astype(jnp.bfloat16), "dp", axis=0, tiled=True).astype(mine.dtype)
     scores = jnp.dot(mine, cands.T, precision=hi, preferred_element_type=jnp.float32) / 0.05

time: 437 us -> 398 us (0.911)
  blocking collectives: 58.9 us -> 19.6 us
    psum x1 -> x0, blocking collectives: 58.9 us -> none  [on_device(): summed = lax.psum(pooled.astype(jnp.bfloat16), 'ctx').astype(jnp.float32)]
    all_gather x0 -> x1, blocking collectives: none -> 19.6 us  [on_device(): lax.all_gather(pooled.astype(jnp.bfloat16), 'ctx')]
where the time goes in v1:
time: 398 us; the launch traced here: 396 us
  other arithmetic  168 us (42%)
  waiting for transfers between devices  94.5 us (24%)
  matrix products  61.9 us (16%)
  local copies, waits for them, and re-layouts  33 us (8%)
  blocking collectives  19.6 us (5%)
  between operations  14.4 us (4%)
  starting transfers between devices  4.72 us (1%)
    another operation x4, other arithmetic, on_device(): jax.scipy.linalg.solve_triangular(system, rhs, lower=True, unit_diagonal=...  159 us
    all_gather x2, waiting for transfers between devices, entering(): lax.all_gather(part.astype(kind), axis)  94.5 us
    dot_general x16, matrix products, combine(): jnp.einsum('hij,hjk->hik', later[0], earlier[1], precision=hi) + later[1]  36.7 us
    all_gather x1, blocking collectives, on_device(): lax.all_gather(pooled.astype(jnp.bfloat16), 'ctx')  19.6 us
    while x16, local copies, waits for them, and re-layouts  16.7 us
    another operation x10, local copies, waits for them, and re-layouts  8.5 us
  transfers between devices with their start and end apart: 4, of which 2 were waited for; matrix products, arithmetic and copies ran while one was open for 4% of the time, Pallas kernels for 0%

profile of v1, /device:TPU:0, one launch (start us, length us, event | category | flops | bytes accessed | tf_op | source)
XLA Modules:
  0.0 396.3 jit_solution(17490308774528419857)
XLA Ops:
  7.2 1.3 slice.54
  8.5 2.9 collective-permute-start
  11.5 1.2 copy.48
  14.1 0.7 iota_compare_fusion.2
  15.1 1.2 copy.51
  16.3 1.6 bitcast_multiply_fusion.1
  17.9 0.8 compare_convert_fusion.1
  19.5 1.7 select_exponential_fusion
  21.2 4.0 select_add_fusion
  25.2 8.1 %while.15 = (s32[]{:T(128)}, f32[8,256,256]{2,1,0:T(8,128)}, s32[2,2]{1,0:T(2,128)S(1)}, f32[2,8,128,128]{3,2,0,1:T(8,128)}, s32[]{:T(128)}) while((s32[]{:T(128)}, f32[8,256,256]{2,1,0:T(8,128)}, s32[2,2]{1,0:T(2,128)S(1)}, f32[2,8,128,128]{3,2,0,1:T(8,128)}, s32[]{:T(128)}) %tuple.61), condition=%wide.while_cond, body=%wide.while_body.sunk | while | flops 2 | bytes 1050209 | solution.py:76
  25.8 3.6 bitcast_dynamic-update-slice_fusion.2
  30.0 3.4 bitcast_dynamic-update-slice_fusion.2
  33.4 158.6 %custom-call.4 = f32[8,2,128,128]{2,3,1,0:T(8,128)} custom-call(f32[8,2,128,128]{3,2,1,0:T(8,128)} %bitcast.137), custom_call_target="InvertDiagBlocksLowerTriangular" | custom-call | tf_op jit(solution)/shard_map/jit(_solve_triangular)/vmap()/triangular_solve | solution.py:76
  192.6 0.6 copy-done.6
  193.2 1.0 fusion.13
  194.3 2.1 convolution_subtract_fusion.1
  196.4 1.0 fusion.33
  197.4 0.8 slice.79
  198.3 3.4 convolution_convert_fusion
  202.1 3.4 fusion.10
  205.5 1.1 convert_bitcast_fusion
  207.2 0.6 copy-done.1
  207.8 3.3 fusion.25
  211.2 43.2 %all-gather.8.cloned.1.call-done = bf16[128,128,128]{2,1,0:T(8,128)(2,1)} async-done(((bf16[8,128,128]{2,1,0:T(8,128)(2,1)}), bf16[128,128,128]{2,1,0:T(8,128)(2,1)}) %all-gather.8.cloned.1.call-update) | async-done | bytes 4194320 | tf_op jit(solution)/shard_map/all_gather | solution.py:16
  254.4 51.2 %all-gather.6.cloned.1.call-done = bf16[128,128,128]{2,1,0:T(8,128)(2,1)} async-done(((bf16[8,128,128]{2,1,0:T(8,128)(2,1)}), bf16[128,128,128]{2,1,0:T(8,128)(2,1)}) %all-gather.6.cloned.1.call-update) | async-done | bytes 4194320 | tf_op jit(solution)/shard_map/all_gather | solution.py:16
  305.6 53.4 %while.16 = (s32[]{:T(128)}, f32[8,128,128]{2,1,0:T(8,128)}, s32[]{:T(128)}, bf16[16,8,128,128]{3,2,1,0:T(8,128)(2,1)}, bf16[16,8,128,128]{3,2,1,0:T(8,128)(2,1)}, /*index=5*/s32[]{:T(128)}, s32[]{:T(128)}) while((s32[]{:T(128)}, f32[8,128,128]{2,1,0:T(8,128)}, s32[]{:T(128)}, bf16[16,8,128,128]{3,2,1,0:T(8,128)(2,1)}, ...), condition=%wide.region_7.8_spmd.clone, body=%wide.region_6.7_spmd.clone.sunk | while | flops 201981952 | bytes 3148383 | solution.py:33
  305.6 1.0 copy.102
  306.7 2.3 fusion.72
  309.0 1.0 copy.102
  310.0 2.3 fusion.72
  312.3 1.0 copy.102
  313.3 2.3 fusion.72
  315.6 1.0 copy.102
  316.7 2.3 fusion.72
  319.0 1.0 copy.102
  320.0 2.3 fusion.72
  322.3 1.0 copy.102
  323.4 2.3 fusion.72
  325.6 1.0 copy.102
  326.7 2.3 fusion.72
  329.0 1.0 copy.102
  330.0 2.3 fusion.72
  332.3 1.0 copy.102
  333.4 2.3 fusion.72
  335.7 1.0 copy.102
  336.7 2.3 fusion.72
  339.0 1.0 copy.102
  340.0 2.3 fusion.72
  342.3 1.0 copy.102
  343.4 2.3 fusion.72
  345.7 1.0 copy.102
  346.7 2.3 fusion.72
  349.0 1.0 copy.102
  350.0 2.3 fusion.72
  352.3 1.0 copy.102
  353.4 2.3 fusion.72
  355.7 1.0 copy.102
  356.7 2.3 fusion.72
  359.0 2.2 convolution_subtract_fusion
  361.3 1.5 fusion.26
  362.9 2.8 multiply_reduce_fusion
  366.2 1.5 collective-permute-start.1
  367.9 19.6 %all-gather.2 = bf16[128,1024]{1,0:T(8,128)(2,1)S(1)} all-gather(bf16[8,1024]{1,0:T(8,128)(2,1)S(1)} %convolution_convert_fusion.1), channel_id=4, replica_groups=mesh['groups'=1,'ctx'=16,'pipe'=2,'dp'=1] {'ctx'}, dimensions={0}, use_global_device_ids=true | all-gather | bytes 278528 | tf_op jit(solution)/shard_map/all_gather | solution.py:108
  388.5 1.0 copy.58
  (74 shorter events, 7.0 us)
Async XLA Ops:
  7.2 6.2 %copy-start.12 = (f32[1,1,8,256]{3,2,1,0:T(8,128)S(1)}, f32[1,1,8,256]{3,2,1,0:T(8,128)}, u32[]{:S(2)}) copy-start(f32[1,1,8,256]{3,2,1,0:T(8,128)} %param.14) | copy-start | bytes 24580
  7.2 7.7 %copy-start.7 = (bf16[1,1,256,1024]{3,2,1,0:T(8,128)(2,1)S(1)}, bf16[1,1,256,1024]{3,2,1,0:T(8,128)(2,1)}, u32[]{:S(2)}) copy-start(bf16[1,1,256,1024]{3,2,1,0:T(8,128)(2,1)} %param.10) | copy-start | bytes 1572868
  7.2 247.2 %all-gather.8.cloned.1.call-start = ((), (), s32[]{:S(2)}) async-start(), calls=%async_computation.1 | async-start | bytes 4456448 | tf_op jit(solution)/shard_map/all_gather | solution.py:16
  8.5 9.4 %collective-permute-start = (s32[1]{0:T(128)}, s32[1]{0:T(128)}, u32[]{:S(2)}, u32[]{:S(2)}) collective-permute-start(s32[1]{0:T(128)} %bitcast.4), channel_id=1, source_target_pairs={{0,2},{2,4},{4,6},{6,8},{8,10},{10,12},{12,14},{14,16},{16,18},{18... | collective-permute-start | bytes 20 | tf_op jit(solution)/shard_map/ppermute | solution.py:10
  13.0 3.3 copy-start.10
  15.1 6.1 %copy-start.4 = (bf16[1,1,256,1024]{2,3,1,0:T(8,128)(2,1)}, bf16[1,1,256,1024]{2,3,1,0:T(8,128)(2,1)S(1)}, u32[]{:S(2)}) copy-start(bf16[1,1,256,1024]{2,3,1,0:T(8,128)(2,1)S(1)} %copy.46) | copy-start | bytes 1572868
  15.1 2.8 copy-start.11
  16.3 4.9 %copy-start.8 = (pred[256,256]{1,0:T(8,128)(4,1)S(1)}, pred[256,256]{1,0:T(8,128)(4,1)}, u32[]{:S(2)}) copy-start(pred[256,256]{1,0:T(8,128)(4,1)} %get-tuple-element.159) | copy-start | bytes 196612
  16.3 4.9 %copy-start.9 = (pred[256,256]{1,0:T(8,128)(4,1)S(1)}, pred[256,256]{1,0:T(8,128)(4,1)}, u32[]{:S(2)}) copy-start(pred[256,256]{1,0:T(8,128)(4,1)} %get-tuple-element.160) | copy-start | bytes 196612
  192.0 1.2 copy-start.6
  201.7 104.0 %all-gather.6.cloned.1.call-start = ((), (), s32[]{:S(2)}) async-start(), calls=%async_computation | async-start | bytes 4456448 | tf_op jit(solution)/shard_map/all_gather | solution.py:16
  206.9 1.0 copy-start.1
  359.0 2.3 copy-start
  359.0 2.3 copy-start.2
  361.3 1.6 copy-start.3
  362.9 2.9 copy-start.5
  362.9 2.9 copy-start.13
  365.7 22.0 %copy-start.14 = (s32[1,1,8]{2,1,0:T(1,128)S(1)}, s32[1,1,8]{2,1,0:T(1,128)}, u32[]{:S(2)}) copy-start(s32[1,1,8]{2,1,0:T(1,128)} %param.16) | copy-start | bytes 100
  366.2 22.3 %collective-permute-start.1 = (bf16[256,1024]{0,1:T(8,128)(2,1)S(1)}, bf16[256,1024]{0,1:T(8,128)(2,1)S(1)}, u32[]{:S(2)}, u32[]{:S(2)}) collective-permute-start(bf16[256,1024]{0,1:T(8,128)(2,1)S(1)} %bitcast.123), channel_id=1, source_target_pairs={{0,1},{1,0},{2,3},{3,2},{4,5},{5,4},{6,7},{7,6},{8,9},{9,8},{10,11... | collective-permute-start | bytes 1572872 | tf_op jit(solution)/shard_map/ppermute | solution.py:38
Sparse Core Ops, SparseCore 0:
  201.8 52.5 all-gather.7
  256.6 49.0 all-gather.5
